TPU v7x, 128 devices: a whole 4x4x4 slice. The times are simulated.
128 devices in a mesh: ctx: 8 (over z, x_hi), fsdp: 16 (over y, x_lo, core).
Axes of the slice: x: 4 (x_hi: 2, x_lo: 2; x = x_hi * 2 + x_lo), y: 4, z: 4, core: 2. Of those that a mesh axis runs over, the one named last changes fastest.
Arguments:
- queries: bfloat16 [16, 2048, 2048], P('fsdp', 'ctx'), may hold values from -36 to 36
- keys: bfloat16 [16, 2048, 512], P('fsdp', 'ctx'), may hold values from -6 to 6
- values: bfloat16 [16, 2048, 512], P('fsdp', 'ctx'), may hold values from -6 to 6
- resid: bfloat16 [16, 2048, 2048], P('fsdp', 'ctx'), may hold values from -6 to 6
- grad_out: bfloat16 [16, 2048, 2048], P('fsdp', 'ctx'), may hold values from -8 to 8
- w_out: bfloat16 [2048, 2048], P(None, 'fsdp'), may hold values from -0.125 to 0.125
- block_list: int32 [16, 8], P('ctx'), may hold values from 0 to 15, as said below
- block_count: int32 [16], P('ctx'), may hold values from 1 to 8, as said below
Outputs:
- mixed: bfloat16 [16, 2048, 2048], P('fsdp', 'ctx')
- query_grad: bfloat16 [16, 2048, 2048], P('fsdp', 'ctx')
- key_grad: bfloat16 [16, 2048, 512], P('fsdp', 'ctx')
- value_grad: bfloat16 [16, 2048, 512], P('fsdp', 'ctx')
- proj_grad: float32 [2048, 2048], P('ctx', 'fsdp')
Inputs may be any that keep to these rules, and one draw needn't show every extreme that they name: `block_list`: row r lists the key blocks of query block r within its sequence: entry 0 is r itself; entries 1 to block_count[r] - 1 are distinct blocks before r; entries from block_count[r] on are ignored and hold r or earlier blocks. block_count[r] is at most min(r + 1, 8); the last query block has exactly 8.
All inputs are finite; a program needn't handle non-finite values.
Results may differ from a plain program's by a relative error of at most 0.025.
Values may be sent and summed in bfloat16 or wider, within the bound.
A program may use at most 192 MiB of HBM per device.

v0:
```python
import math
import jax
import jax.numpy as jnp
from jax import lax
from jax.sharding import PartitionSpec as P

QUERY_HEADS = 16
KEY_VALUE_HEADS = 4
HEAD_DIM = 128
BLOCK_SIZE = 128
KEY_SLOTS = 8


def score_mask(first_row, listed_blocks, live_count):
    query_pos = first_row + jnp.arange(BLOCK_SIZE, dtype=jnp.int32)
    key_pos = listed_blocks[:, None] * BLOCK_SIZE + jnp.arange(BLOCK_SIZE, dtype=jnp.int32)[None, :]
    slot_live = jnp.arange(KEY_SLOTS, dtype=jnp.int32) < live_count
    return (key_pos[None, :, :] <= query_pos[:, None, None]) & slot_live[None, :, None]


def block_weights(query_blk, key_sel, allowed):
    scale = 1.0 / math.sqrt(HEAD_DIM)
    scores = (
        jnp.einsum("qgrd,sbgd->grqsb", query_blk, key_sel, preferred_element_type=jnp.float32)
        * scale
    )
    scores = jnp.where(allowed[None, None], scores, jnp.float32(-1e30))
    top = jnp.max(scores, axis=(3, 4), keepdims=True)
    expon = jnp.exp(scores - top)
    probs = expon / jnp.sum(expon, axis=(3, 4), keepdims=True)
    return (probs, probs.astype(jnp.bfloat16))


def local(queries, keys, values, resid, grad_out, w_out, block_list, block_count):
    scale = 1.0 / math.sqrt(HEAD_DIM)
    query_groups = QUERY_HEADS // KEY_VALUE_HEADS
    seq_rows = queries.shape[1]
    device_local_blocks = seq_rows // BLOCK_SIZE
    first_block = lax.axis_index("ctx") * device_local_blocks
    block_pos = first_block + jnp.arange(device_local_blocks, dtype=jnp.int32)
    complete_keys, complete_values = (
        lax.all_gather(keys, "ctx", axis=1, tiled=True),
        lax.all_gather(values, "ctx", axis=1, tiled=True),
    )
    block_total = complete_keys.shape[1] // BLOCK_SIZE
    blocked_keys = complete_keys[0].reshape(block_total, BLOCK_SIZE, KEY_VALUE_HEADS, HEAD_DIM)
    blocked_values = complete_values[0].reshape(block_total, BLOCK_SIZE, KEY_VALUE_HEADS, HEAD_DIM)
    blocked_queries = queries[0].reshape(
        device_local_blocks, BLOCK_SIZE, KEY_VALUE_HEADS, query_groups, HEAD_DIM
    )

    def forward_block(operands):
        query_blk, listed_blocks, live_count, position = operands
        allowed = score_mask(position * BLOCK_SIZE, listed_blocks, live_count)
        key_sel = jnp.take(blocked_keys, listed_blocks, axis=0)
        value_sel = jnp.take(blocked_values, listed_blocks, axis=0)
        probs, probs_b = block_weights(query_blk, key_sel, allowed)
        attended = jnp.einsum(
            "grqsb,sbgd->qgrd", probs_b, value_sel, preferred_element_type=jnp.float32
        )
        return attended.astype(jnp.bfloat16)

    out_blocks = lax.map(forward_block, (blocked_queries, block_list, block_count, block_pos))
    out_rows = out_blocks.reshape(seq_rows, QUERY_HEADS * HEAD_DIM)
    grad_rows = grad_out[0]
    w_whole = lax.all_gather(w_out, "fsdp", axis=1, tiled=True)
    projected = jnp.dot(out_rows, w_whole, preferred_element_type=jnp.float32)
    attended_gradient = lax.dot_general(
        grad_rows, w_whole, (((1,), (1,)), ((), ())), preferred_element_type=jnp.float32
    )
    mixed = (resid[0].astype(jnp.float32) + projected).astype(jnp.bfloat16)
    output_grad_blocks = attended_gradient.astype(jnp.bfloat16).reshape(
        device_local_blocks, BLOCK_SIZE, KEY_VALUE_HEADS, query_groups, HEAD_DIM
    )

    def backward_block(operands):
        query_blk, out_blk, dout_blk, listed_blocks, live_count, position = operands
        allowed = score_mask(position * BLOCK_SIZE, listed_blocks, live_count)
        key_sel = jnp.take(blocked_keys, listed_blocks, axis=0)
        value_sel = jnp.take(blocked_values, listed_blocks, axis=0)
        probs, probs_b = block_weights(query_blk, key_sel, allowed)
        value_part = jnp.einsum(
            "grqsb,qgrd->sbgd", probs_b, dout_blk, preferred_element_type=jnp.float32
        )
        prob_grads = jnp.einsum(
            "qgrd,sbgd->grqsb", dout_blk, value_sel, preferred_element_type=jnp.float32
        )
        row_dot = jnp.sum(dout_blk.astype(jnp.float32) * out_blk.astype(jnp.float32), axis=-1)
        row_dot = jnp.transpose(row_dot, (1, 2, 0))[:, :, :, None, None]
        score_grads = (probs * (prob_grads - row_dot) * scale).astype(jnp.bfloat16)
        query_part = jnp.einsum(
            "grqsb,sbgd->qgrd", score_grads, key_sel, preferred_element_type=jnp.float32
        ).astype(jnp.bfloat16)
        key_part = jnp.einsum(
            "grqsb,qgrd->sbgd", score_grads, query_blk, preferred_element_type=jnp.float32
        )
        return (query_part, key_part, value_part)

    query_parts, key_fragments, value_fragments = lax.map(
        backward_block,
        (blocked_queries, out_blocks, output_grad_blocks, block_list, block_count, block_pos),
    )
    listed_all = block_list.reshape(-1)
    key_holder = (
        jnp.zeros((block_total, BLOCK_SIZE, KEY_VALUE_HEADS * HEAD_DIM), jnp.float32)
        .at[listed_all]
        .add(
            key_fragments.reshape(
                device_local_blocks * KEY_SLOTS, BLOCK_SIZE, KEY_VALUE_HEADS * HEAD_DIM
            )
        )
    )
    value_holder = (
        jnp.zeros((block_total, BLOCK_SIZE, KEY_VALUE_HEADS * HEAD_DIM), jnp.float32)
        .at[listed_all]
        .add(
            value_fragments.reshape(
                device_local_blocks * KEY_SLOTS, BLOCK_SIZE, KEY_VALUE_HEADS * HEAD_DIM
            )
        )
    )
    key_sum, value_sum = (
        lax.psum_scatter(
            key_holder.reshape(1, block_total * BLOCK_SIZE, KEY_VALUE_HEADS * HEAD_DIM).astype(
                jnp.bfloat16
            ),
            "ctx",
            scatter_dimension=1,
            tiled=True,
        ).astype(jnp.float32),
        lax.psum_scatter(
            value_holder.reshape(1, block_total * BLOCK_SIZE, KEY_VALUE_HEADS * HEAD_DIM).astype(
                jnp.bfloat16
            ),
            "ctx",
            scatter_dimension=1,
            tiled=True,
        ).astype(jnp.float32),
    )
    feature_share = lax.psum_scatter(
        lax.dot_general(
            grad_rows, out_rows, (((0,), (0,)), ((), ())), preferred_element_type=jnp.float32
        ).astype(jnp.bfloat16),
        "fsdp",
        scatter_dimension=0,
        tiled=True,
    )
    proj_grad = (
        lax.psum_scatter(feature_share, "ctx", scatter_dimension=1, tiled=True)
        .astype(jnp.float32)
        .T
    )
    query_grad = query_parts.reshape(1, seq_rows, QUERY_HEADS * HEAD_DIM)
    return (
        mixed[None],
        query_grad,
        key_sum.astype(jnp.bfloat16),
        value_sum.astype(jnp.bfloat16),
        proj_grad,
    )


def solution(mesh):
    in_specs = (
        P("fsdp", "ctx", None),
        P("fsdp", "ctx", None),
        P("fsdp", "ctx", None),
        P("fsdp", "ctx", None),
        P("fsdp", "ctx", None),
        P(None, "fsdp"),
        P("ctx", None),
        P("ctx"),
    )
    out_specs = (
        P("fsdp", "ctx", None),
        P("fsdp", "ctx", None),
        P("fsdp", "ctx", None),
        P("fsdp", "ctx", None),
        P("ctx", "fsdp"),
    )
    return jax.shard_map(local, mesh=mesh, in_specs=in_specs, out_specs=out_specs, check_vma=False)
```

profile of v0, /device:TPU:0, one launch (start us, length us, event | category | flops | bytes accessed | tf_op | source)
XLA Modules:
  0.0 542.2 jit_solution(563951076636998370)
XLA Ops:
  12.5 54.5 %all-gather.4.cloned.1.call-done = bf16[1,2048,512]{2,1,0:T(8,128)(2,1)} async-done(((bf16[1,256,512]{2,1,0:T(8,128)(2,1)}), bf16[1,2048,512]{2,1,0:T(8,128)(2,1)}) %all-gather.4.cloned.1.call-update) | async-done | bytes 2097168 | tf_op jit(solution)/shard_map/all_gather | solution.py:43
  67.0 4.0 reshape_squeeze.9
  71.0 50.3 %all-gather.6.cloned.1.call-done = bf16[1,2048,512]{2,1,0:T(8,128)(2,1)} async-done(((bf16[1,256,512]{2,1,0:T(8,128)(2,1)}), bf16[1,2048,512]{2,1,0:T(8,128)(2,1)}) %all-gather.6.cloned.1.call-update) | async-done | bytes 2097168 | tf_op jit(solution)/shard_map/all_gather | solution.py:42
  121.3 4.0 reshape_squeeze.10
  125.3 35.7 %while.24 = (s32[]{:T(128)}, bf16[2,128,4,4,128]{1,4,3,2,0:T(8,128)(2,1)}, s32[2,8]{1,0:T(2,128)S(1)}, bf16[16,128,4,128]{3,2,1,0:T(4,128)(2,1)}, s32[2]{0:T(128...) while((s32[]{:T(128)}, ...), condition=%wide.region_3.5_spmd, body=%wide.region_0.4_spmd.sunk | while | flops 1100478720 | bytes 45667840 | solution.py:63
  125.3 3.0 gather_fusion
  128.4 3.0 gather_fusion.1
  143.1 3.0 gather_fusion
  146.1 3.2 gather_fusion.1
  163.9 5.6 %convert_bitcast_fusion = bf16[2048,2048]{0,1:T(8,128)(2,1)} fusion(bf16[256,2048]{1,0:T(8,128)(2,1)S(1)} %reshape.176, bf16[1,256,2048]{2,1,0:T(8,128)(2,1)S(1)} %copy-done), kind=kOutput, calls=%fused_computation.87 | convolution fusion | flops 2151677952 | bytes 10485760 | tf_op jit(solution)/shard_map/dot_general | solution.py:141
  169.5 12.3 %copy.122 = bf16[2048,2048]{1,0:T(8,128)(2,1)} copy(bf16[2048,2048]{0,1:T(8,128)(2,1)} %convert_bitcast_fusion) | data formatting | bytes 16777216
  182.6 5.7 %convolution_convert_fusion = bf16[256,2048]{1,0:T(8,128)(2,1)S(1)} fusion(bf16[2048,2048]{1,0:T(8,128)(2,1)} %all-gather.8.cloned.1.call-done, bf16[1,256,2048]{2,1,0:T(8,128)(2,1)S(1)} %copy-done), kind=kOutput, calls=%fused_computation.90 | convolution fusion | flops 2148007936 | bytes 10485760 | tf_op jit(solution)/shard_map/dot_general | solution.py:68
  189.9 91.2 %reduce-scatter.13.cloned.1.call-done = bf16[128,2048]{1,0:T(8,128)(2,1)} async-done(((bf16[2048,2048]{1,0:T(8,128)(2,1)}), bf16[128,2048]{1,0:T(8,128)(2,1)}) %reduce-scatter.13.cloned.1.call-update) | async-done | bytes 524304
  283.2 78.1 %while.25 = (s32[]{:T(128)}, bf16[2,128,4,4,128]{4,3,2,1,0:T(4,128)(2,1)}, f32[2,8,128,4,128]{2,4,3,1,0:T(8,128)}, f32[2,8,128,4,128]{2,4,3,1,0:T(8,128)}, s32[2...) while((s32[]{:T(128)}, ...), condition=%wide.region_8.10_spmd, body=%wide.region_4.9_spmd.sunk | while | flops 2728915200 | bytes 224614144 | solution.py:99
  283.2 3.0 gather_fusion.2
  286.3 3.0 gather_fusion.3
  297.9 2.6 fusion.107
  302.3 3.4 fusion.109
  310.0 5.0 fusion.111
  322.3 3.0 gather_fusion.2
  325.4 3.0 gather_fusion.3
  341.4 3.4 fusion.109
  349.1 5.0 fusion.111
  361.3 5.4 copy.85
  369.2 9.4 %scatter_fusion = f32[16,128,512]{2,1,0:T(8,128)} fusion(f32[16,128,512]{2,1,0:T(8,128)} %broadcast.137.clone, s32[16]{0:T(128)S(1)} %copy-done.17, f32[16,128,512]{2,1,0:T(8,128)} %copy.85), kind=kCustom, calls=%fused_computation.4 | custom fusion | flops 1048576 | bytes 12582976 | tf_op jit(solution)/shard_map/scatter-add | solution.py:107
  378.6 3.8 convert_element_type.85
  382.5 5.4 copy.87
  390.3 9.4 %scatter_fusion.1 = f32[16,128,512]{2,1,0:T(8,128)} fusion(f32[16,128,512]{2,1,0:T(8,128)} %broadcast.137.clone.1, s32[16]{0:T(128)S(1)} %copy-done.17, f32[16,128,512]{2,1,0:T(8,128)} %copy.87), kind=kCustom, calls=%fused_computation.5 | custom fusion | flops 1048576 | bytes 12582976 | tf_op jit(solution)/shard_map/scatter-add | solution.py:116
  399.8 4.0 convert_element_type.87
  405.4 7.0 %fusion.64 = bf16[1,256,2048]{2,1,0:T(8,128)(2,1)} fusion(bf16[256,2048]{1,0:T(8,128)(2,1)S(1)} %copy-done.10, bf16[2048,2048]{1,0:T(8,128)(2,1)} %all-gather.8.cloned.1.call-done, bf16[1,256,2048]{2,1,0:T(8,128)(2,1)} %param.17), kind=kOutput, calls=%fused_computation.91 | convolution fusion | flops 2149056512 | bytes 11534336 | tf_op jit(solution)/shard_map/dot_general | solution.py:67
  413.9 42.8 %reduce-scatter.7.cloned.1.call-done = bf16[1,256,512]{2,1,0:T(8,128)(2,1)} async-done(((bf16[1,2048,512]{2,1,0:T(8,128)(2,1)}), bf16[1,256,512]{2,1,0:T(8,128)(2,1)}) %reduce-scatter.7.cloned.1.call-update) | async-done | bytes 262160 | tf_op jit(solution)/shard_map/reduce_scatter | solution.py:123
  456.7 78.6 %reduce-scatter.9.cloned.1.call-done = bf16[1,256,512]{2,1,0:T(8,128)(2,1)} async-done(((bf16[1,2048,512]{2,1,0:T(8,128)(2,1)}), bf16[1,256,512]{2,1,0:T(8,128)(2,1)}) %reduce-scatter.9.cloned.1.call-update) | async-done | bytes 262160 | tf_op jit(solution)/shard_map/reduce_scatter | solution.py:131
  (162 shorter events, 87.4 us)
Async XLA Ops:
  7.2 156.7 %copy-start = (bf16[1,256,2048]{2,1,0:T(8,128)(2,1)S(1)}, bf16[1,256,2048]{2,1,0:T(8,128)(2,1)}, u32[]{:S(2)}) copy-start(bf16[1,256,2048]{2,1,0:T(8,128)(2,1)} %param.18) | copy-start | bytes 3145732
  7.2 118.1 %copy-start.16 = (s32[2,8]{1,0:T(2,128)S(1)}, s32[2,8]{1,0:T(2,128)}, u32[]{:S(2)}) copy-start(s32[2,8]{1,0:T(2,128)} %param.20) | copy-start | bytes 196
  7.2 118.1 %copy-start.18 = (s32[2]{0:T(128)S(1)}, s32[2]{0:T(128)}, u32[]{:S(2)}) copy-start(s32[2]{0:T(128)} %param.21) | copy-start | bytes 28
  7.2 59.8 %all-gather.4.cloned.1.call-start = ((), (), s32[]{:S(2)}) async-start(), calls=%async_computation.4 | async-start | bytes 2359296 | tf_op jit(solution)/shard_map/all_gather | solution.py:43
  7.9 113.4 %all-gather.6.cloned.1.call-start = ((), (), s32[]{:S(2)}) async-start(), calls=%async_computation.5 | async-start | bytes 2359296 | tf_op jit(solution)/shard_map/all_gather | solution.py:42
  8.7 173.9 %all-gather.8.cloned.1.call-start = ((), (), s32[]{:S(2)}) async-start(), calls=%async_computation.6 | async-start | bytes 8912896 | tf_op jit(solution)/shard_map/all_gather | solution.py:66
  9.4 271.6 %reduce-scatter.13.cloned.1.call-start = ((), (), s32[]{:S(2)}) async-start(), calls=%async_computation.10 | async-start | bytes 8912896
  135.2 4.3 copy-start.7
  153.1 4.3 copy-start.7
  163.9 18.0 %copy-start.9 = (bf16[256,2048]{1,0:T(8,128)(2,1)}, bf16[256,2048]{1,0:T(8,128)(2,1)S(1)}, u32[]{:S(2)}) copy-start(bf16[256,2048]{1,0:T(8,128)(2,1)S(1)} %reshape.176) | copy-start | bytes 3145732
  181.9 230.5 %reduce-scatter.11.cloned.1.call-start = ((), (), s32[]{:S(2)}) async-start(), calls=%async_computation.9 | async-start | bytes 589824 | tf_op jit(solution)/shard_map/reduce_scatter | solution.py:149
  283.1 173.6 %reduce-scatter.7.cloned.1.call-start = ((), (), s32[]{:S(2)}) async-start(), calls=%async_computation.7 | async-start | bytes 2359296 | tf_op jit(solution)/shard_map/reduce_scatter | solution.py:123
  297.9 4.4 copy-start.6
  300.6 5.2 copy-start.2
  305.7 2.0 copy-start.3
  310.0 5.0 copy-start.4
  310.0 5.0 copy-start.5
  314.9 2.2 copy-start.11
  314.9 3.5 copy-start.13
  319.0 3.2 copy-start.14
  337.0 4.4 copy-start.6
  339.6 5.2 copy-start.2
  349.1 5.0 copy-start.4
  349.1 5.0 copy-start.5
  354.0 2.2 copy-start.11
  354.0 3.4 copy-start.13
  358.1 3.2 copy-start.14
  361.3 7.9 %copy-start.17 = (s32[16]{0:T(128)S(1)}, s32[16]{0:T(128)}, u32[]{:S(2)}) copy-start(s32[16]{0:T(128)} %fusion.67) | copy-start | bytes 196
  382.4 152.9 %reduce-scatter.9.cloned.1.call-start = ((), (), s32[]{:S(2)}) async-start(), calls=%async_computation.8 | async-start | bytes 2359296 | tf_op jit(solution)/shard_map/reduce_scatter | solution.py:131
  390.3 13.4 %copy-start.15 = (bf16[2,128,4,4,128]{4,3,2,1,0:T(4,128)(2,1)S(1)}, bf16[2,128,4,4,128]{4,3,2,1,0:T(4,128)(2,1)}, u32[]{:S(2)}) copy-start(bf16[2,128,4,4,128]{4,3,2,1,0:T(4,128)(2,1)} %get-tuple-element.113) | copy-start | bytes 3145732
  399.7 5.6 %copy-start.10 = (bf16[256,2048]{1,0:T(8,128)(2,1)S(1)}, bf16[256,2048]{1,0:T(8,128)(2,1)}, u32[]{:S(2)}) copy-start(bf16[256,2048]{1,0:T(8,128)(2,1)} %copy-done.9) | copy-start | bytes 3145732
  403.7 131.6 %copy-start.1 = (bf16[1,256,2048]{2,1,0:T(8,128)(2,1)S(1)}, bf16[1,256,2048]{2,1,0:T(8,128)(2,1)}, u32[]{:S(2)}) copy-start(bf16[1,256,2048]{2,1,0:T(8,128)(2,1)} %param.18) | copy-start | bytes 3145732
  (5 other events, 7.9 us)
Sparse Core Ops, SparseCore 0:
  10.4 56.5 all-gather.3
  69.4 51.8 all-gather.5
  123.0 58.0 all-gather.7
  183.3 97.6 reduce-scatter.12
  284.4 69.2 reduce-scatter.10
  382.6 74.0 reduce-scatter.6
  461.4 73.8 reduce-scatter.8
where the time goes:
time: 544 us; the launch traced here: 542 us
  waiting for transfers between devices  320 us (59%)
  local copies, waits for them, and re-layouts  103 us (19%)
  matrix products  55.3 us (10%)
  other arithmetic  46.2 us (8%)
  between operations  14.3 us (3%)
    unnamed x8, waiting for transfers between devices  93.3 us
    reduce_scatter x1, waiting for transfers between devices, local(): lax.psum_scatter(value_holder.reshape(1, block_total * BLOCK_SIZE, KEY_VA...  78.6 us
    all_gather x1, waiting for transfers between devices, local(): lax.all_gather(values, 'ctx', axis=1, tiled=True)  54.5 us
    all_gather x1, waiting for transfers between devices, local(): lax.all_gather(keys, 'ctx', axis=1, tiled=True)  50.3 us
    reduce_scatter x1, waiting for transfers between devices, local(): lax.psum_scatter(key_holder.reshape(1, block_total * BLOCK_SIZE, KEY_VALU...  42.8 us
    while x44, local copies, waits for them, and re-layouts  16.2 us
    unnamed x18, local copies, waits for them, and re-layouts  14.4 us
  transfers between devices with their start and end apart: 7, of which 5 were waited for; matrix products, arithmetic and copies ran while one was open for 34% of the time, Pallas kernels for 0%

commit v1 on v0

--- a/solution.py
+++ b/solution.py
@@ -40,7 +40,9 @@
     block_pos = first_block + jnp.arange(device_local_blocks, dtype=jnp.int32)
     complete_keys, complete_values = (
         lax.all_gather(keys, "ctx", axis=1, tiled=True),
-        lax.all_gather(values, "ctx", axis=1, tiled=True),
+        jnp.concatenate(
+            lax.all_to_all(jnp.stack([values] * lax.axis_size("ctx")), "ctx", 0, 0), axis=1
+        ),
     )
     block_total = complete_keys.shape[1] // BLOCK_SIZE
     blocked_keys = complete_keys[0].reshape(block_total, BLOCK_SIZE, KEY_VALUE_HEADS, HEAD_DIM)

time: 544 us -> 501 us (0.921)
  waiting for transfers between devices: 320 us -> 267 us
  starting transfers between devices: 0.28 us -> 8.41 us
    all_gather x1 -> x0, waiting for transfers between devices: 54.5 us -> none  [local(): lax.all_gather(values, 'ctx', axis=1, tiled=True)]
    all_to_all x0 -> x1, waiting for transfers between devices: none -> 26.1 us  [local(): lax.all_to_all(jnp.stack([values] * lax.axis_size('ctx')), 'ctx', 0, 0)]
    all_gather x1, waiting for transfers between devices: 50.3 us -> 26.7 us  [local(): lax.all_gather(keys, 'ctx', axis=1, tiled=True)]
    all_to_all x0 -> x1, starting transfers between devices: none -> 7.99 us  [local(): lax.all_to_all(jnp.stack([values] * lax.axis_size('ctx')), 'ctx', 0, 0)]
    unnamed x8 -> x7, waiting for transfers between devices: 93.3 us -> 92.5 us
  transfers between devices with their start and end apart: 7 -> 7, of which waited for: 5 -> 5; matrix products, arithmetic and copies ran while one was open for 34% -> 38% of each run, Pallas kernels for 0% -> 0%
where the time goes in v1:
time: 501 us; the launch traced here: 500 us
  waiting for transfers between devices  267 us (53%)
  local copies, waits for them, and re-layouts  106 us (21%)
  matrix products  55.3 us (11%)
  other arithmetic  45.8 us (9%)
  between operations  14.2 us (3%)
  starting transfers between devices  8.41 us (2%)
    unnamed x7, waiting for transfers between devices  92.5 us
    reduce_scatter x1, waiting for transfers between devices, local(): lax.psum_scatter(value_holder.reshape(1, block_total * BLOCK_SIZE, KEY_VA...  78.5 us
    reduce_scatter x1, waiting for transfers between devices, local(): lax.psum_scatter(key_holder.reshape(1, block_total * BLOCK_SIZE, KEY_VALU...  43.2 us
    all_gather x1, waiting for transfers between devices, local(): lax.all_gather(keys, 'ctx', axis=1, tiled=True)  26.7 us
    all_to_all x1, waiting for transfers between devices, local(): lax.all_to_all(jnp.stack([values] * lax.axis_size('ctx')), 'ctx', 0, 0)  26.1 us
    while x44, local copies, waits for them, and re-layouts  16.1 us
    unnamed x18, local copies, waits for them, and re-layouts  14.6 us
    dot_general x4, matrix products, block_weights(): jnp.einsum('qgrd,sbgd->grqsb', query_blk, key_sel, preferred_element_type...  10.3 us
  transfers between devices with their start and end apart: 7, of which 5 were waited for; matrix products, arithmetic and copies ran while one was open for 38% of the time, Pallas kernels for 0%

profile of v1, /device:TPU:0, one launch (start us, length us, event | category | flops | bytes accessed | tf_op | source)
XLA Modules:
  0.0 499.9 jit_solution(9950152109460023355)
XLA Ops:
  11.1 8.0 %all-to-all-start = ((bf16[8,1,256,512]{3,2,1,0:T(8,128)(2,1)}), bf16[8,1,256,512]{3,2,1,0:T(8,128)(2,1)S(1)}, u32[]{:S(2)}, u32[]{:S(2)}) async-start(bf16[8,1,256,512]{3,2,1,0:T(8,128)(2,1)} %stack.2), calls=%async_computation | async-start | bytes 4194304 | tf_op jit(solution)/shard_map/all_to_all | solution.py:44
  24.3 26.1 %all-to-all-done = bf16[8,1,256,512]{3,2,1,0:T(8,128)(2,1)S(1)} async-done(((bf16[8,1,256,512]{3,2,1,0:T(8,128)(2,1)}), bf16[8,1,256,512]{3,2,1,0:T(8,128)(2,1)S(1)}, u32[]{:S(2)}, u32[]{:S(2)}) %all-to-all-start) | async-done | bytes 2097184 | tf_op jit(solution)/shard_map/all_to_all | solution.py:44
  52.5 26.7 %all-gather.3.cloned.1.call-done = bf16[1,2048,512]{2,1,0:T(8,128)(2,1)} async-done(((bf16[1,256,512]{2,1,0:T(8,128)(2,1)}), bf16[1,2048,512]{2,1,0:T(8,128)(2,1)}) %all-gather.3.cloned.1.call-update) | async-done | bytes 2097168 | tf_op jit(solution)/shard_map/all_gather | solution.py:42
  79.2 4.0 reshape_squeeze.6
  83.1 35.7 %while.24 = (s32[]{:T(128)}, bf16[2,128,4,4,128]{1,4,3,2,0:T(8,128)(2,1)}, s32[2,8]{1,0:T(2,128)S(1)}, bf16[16,128,4,128]{3,2,1,0:T(4,128)(2,1)}, s32[2]{0:T(128...) while((s32[]{:T(128)}, ...), condition=%wide.region_3.5_spmd, body=%wide.region_0.4_spmd.sunk | while | flops 1100478720 | bytes 45667840 | solution.py:65
  83.2 3.0 gather_fusion
  86.2 3.0 gather_fusion.1
  100.9 3.0 gather_fusion
  104.0 3.2 gather_fusion.1
  121.7 5.6 %convert_bitcast_fusion = bf16[2048,2048]{0,1:T(8,128)(2,1)} fusion(bf16[256,2048]{1,0:T(8,128)(2,1)S(1)} %reshape.179, bf16[1,256,2048]{2,1,0:T(8,128)(2,1)S(1)} %copy-done), kind=kOutput, calls=%fused_computation.87 | convolution fusion | flops 2151677952 | bytes 10485760 | tf_op jit(solution)/shard_map/dot_general | solution.py:143
  127.3 12.5 %copy.122 = bf16[2048,2048]{1,0:T(8,128)(2,1)} copy(bf16[2048,2048]{0,1:T(8,128)(2,1)} %convert_bitcast_fusion) | data formatting | bytes 16777216
  140.7 5.7 %convolution_convert_fusion = bf16[256,2048]{1,0:T(8,128)(2,1)S(1)} fusion(bf16[2048,2048]{1,0:T(8,128)(2,1)} %all-gather.5.cloned.1.call-done, bf16[1,256,2048]{2,1,0:T(8,128)(2,1)S(1)} %copy-done), kind=kOutput, calls=%fused_computation.90 | convolution fusion | flops 2148007936 | bytes 10485760 | tf_op jit(solution)/shard_map/dot_general | solution.py:70
  148.0 91.0 %reduce-scatter.13.cloned.1.call-done = bf16[128,2048]{1,0:T(8,128)(2,1)} async-done(((bf16[2048,2048]{1,0:T(8,128)(2,1)}), bf16[128,2048]{1,0:T(8,128)(2,1)}) %reduce-scatter.13.cloned.1.call-update) | async-done | bytes 524304
  241.2 78.1 %while.25 = (s32[]{:T(128)}, bf16[2,128,4,4,128]{4,3,2,1,0:T(4,128)(2,1)}, f32[2,8,128,4,128]{2,4,3,1,0:T(8,128)}, f32[2,8,128,4,128]{2,4,3,1,0:T(8,128)}, s32[2...) while((s32[]{:T(128)}, ...), condition=%wide.region_8.10_spmd, body=%wide.region_4.9_spmd.sunk | while | flops 2728915200 | bytes 224614144 | solution.py:101
  241.2 3.0 gather_fusion.2
  244.2 3.0 gather_fusion.3
  255.9 2.6 fusion.107
  260.3 3.4 fusion.109
  267.9 5.0 fusion.111
  280.3 3.0 gather_fusion.2
  283.3 3.0 gather_fusion.3
  299.4 3.4 fusion.109
  307.0 5.0 fusion.111
  319.2 5.4 %copy.85 = f32[16,128,512]{2,1,0:T(8,128)} copy(f32[16,128,512]{1,2,0:T(8,128)} %bitcast.240) | data formatting | bytes 8388608 | tf_op jit(solution)/shard_map/reshape | solution.py:110
  327.1 9.2 %scatter_fusion = f32[16,128,512]{2,1,0:T(8,128)} fusion(f32[16,128,512]{2,1,0:T(8,128)} %broadcast.140.clone, s32[16]{0:T(128)S(1)} %copy-done.17, f32[16,128,512]{2,1,0:T(8,128)} %copy.85), kind=kCustom, calls=%fused_computation.4 | custom fusion | flops 1048576 | bytes 12582976 | tf_op jit(solution)/shard_map/scatter-add | solution.py:109
  336.3 3.8 convert_element_type.85
  340.2 5.4 %copy.87 = f32[16,128,512]{2,1,0:T(8,128)} copy(f32[16,128,512]{1,2,0:T(8,128)} %bitcast.241) | data formatting | bytes 8388608 | tf_op jit(solution)/shard_map/reshape | solution.py:119
  348.0 9.2 %scatter_fusion.1 = f32[16,128,512]{2,1,0:T(8,128)} fusion(f32[16,128,512]{2,1,0:T(8,128)} %broadcast.140.clone.1, s32[16]{0:T(128)S(1)} %copy-done.17, f32[16,128,512]{2,1,0:T(8,128)} %copy.87), kind=kCustom, calls=%fused_computation.5 | custom fusion | flops 1048576 | bytes 12582976 | tf_op jit(solution)/shard_map/scatter-add | solution.py:118
  357.3 4.0 convert_element_type.87
  362.9 7.0 %fusion.64 = bf16[1,256,2048]{2,1,0:T(8,128)(2,1)} fusion(bf16[256,2048]{1,0:T(8,128)(2,1)S(1)} %copy-done.10, bf16[2048,2048]{1,0:T(8,128)(2,1)} %all-gather.5.cloned.1.call-done, bf16[1,256,2048]{2,1,0:T(8,128)(2,1)} %param.17), kind=kOutput, calls=%fused_computation.91 | convolution fusion | flops 2149056512 | bytes 11534336 | tf_op jit(solution)/shard_map/dot_general | solution.py:69
  371.4 43.2 %reduce-scatter.7.cloned.1.call-done = bf16[1,256,512]{2,1,0:T(8,128)(2,1)} async-done(((bf16[1,2048,512]{2,1,0:T(8,128)(2,1)}), bf16[1,256,512]{2,1,0:T(8,128)(2,1)}) %reduce-scatter.7.cloned.1.call-update) | async-done | bytes 262160 | tf_op jit(solution)/shard_map/reduce_scatter | solution.py:125
  414.6 78.5 %reduce-scatter.9.cloned.1.call-done = bf16[1,256,512]{2,1,0:T(8,128)(2,1)} async-done(((bf16[1,2048,512]{2,1,0:T(8,128)(2,1)}), bf16[1,256,512]{2,1,0:T(8,128)(2,1)}) %reduce-scatter.9.cloned.1.call-update) | async-done | bytes 262160 | tf_op jit(solution)/shard_map/reduce_scatter | solution.py:133
  (162 shorter events, 93.3 us)
Async XLA Ops:
  7.2 114.6 %copy-start = (bf16[1,256,2048]{2,1,0:T(8,128)(2,1)S(1)}, bf16[1,256,2048]{2,1,0:T(8,128)(2,1)}, u32[]{:S(2)}) copy-start(bf16[1,256,2048]{2,1,0:T(8,128)(2,1)} %param.18) | copy-start | bytes 3145732
  7.2 72.0 %all-gather.3.cloned.1.call-start = ((), (), s32[]{:S(2)}) async-start(), calls=%async_computation.5 | async-start | bytes 2359296 | tf_op jit(solution)/shard_map/all_gather | solution.py:42
  7.9 132.8 %all-gather.5.cloned.1.call-start = ((), (), s32[]{:S(2)}) async-start(), calls=%async_computation.6 | async-start | bytes 8912896 | tf_op jit(solution)/shard_map/all_gather | solution.py:68
  11.1 72.0 %copy-start.16 = (s32[2,8]{1,0:T(2,128)S(1)}, s32[2,8]{1,0:T(2,128)}, u32[]{:S(2)}) copy-start(s32[2,8]{1,0:T(2,128)} %param.20) | copy-start | bytes 196
  11.1 72.0 %copy-start.18 = (s32[2]{0:T(128)S(1)}, s32[2]{0:T(128)}, u32[]{:S(2)}) copy-start(s32[2]{0:T(128)} %param.21) | copy-start | bytes 28
  11.1 39.3 %all-to-all-start = ((bf16[8,1,256,512]{3,2,1,0:T(8,128)(2,1)}), bf16[8,1,256,512]{3,2,1,0:T(8,128)(2,1)S(1)}, u32[]{:S(2)}, u32[]{:S(2)}) async-start(bf16[8,1,256,512]{3,2,1,0:T(8,128)(2,1)} %stack.2), calls=%async_computation | async-start | bytes 4194304 | tf_op jit(solution)/shard_map/all_to_all | solution.py:44
  19.1 219.9 %reduce-scatter.13.cloned.1.call-start = ((), (), s32[]{:S(2)}) async-start(), calls=%async_computation.10 | async-start | bytes 8912896
  93.0 4.3 copy-start.7
  111.0 4.3 copy-start.7
  121.7 18.1 %copy-start.9 = (bf16[256,2048]{1,0:T(8,128)(2,1)}, bf16[256,2048]{1,0:T(8,128)(2,1)S(1)}, u32[]{:S(2)}) copy-start(bf16[256,2048]{1,0:T(8,128)(2,1)S(1)} %reshape.179) | copy-start | bytes 3145732
  139.8 230.1 %reduce-scatter.11.cloned.1.call-start = ((), (), s32[]{:S(2)}) async-start(), calls=%async_computation.9 | async-start | bytes 589824 | tf_op jit(solution)/shard_map/reduce_scatter | solution.py:151
  241.1 173.5 %reduce-scatter.7.cloned.1.call-start = ((), (), s32[]{:S(2)}) async-start(), calls=%async_computation.7 | async-start | bytes 2359296 | tf_op jit(solution)/shard_map/reduce_scatter | solution.py:125
  255.9 4.4 copy-start.6
  258.5 5.2 %copy-start.2 = (f32[4,8,128,128,4]{3,2,4,1,0:T(8,128)}, f32[4,8,128,128,4]{3,2,4,1,0:T(8,128)S(1)}, u32[]{:S(2)}) copy-start(f32[4,8,128,128,4]{3,2,4,1,0:T(8,128)S(1)} %get-tuple-element.387) | copy-start | bytes 25165828 | tf_op jit(solution)/shard_map/while
  263.7 2.0 copy-start.3
  267.9 5.0 copy-start.4
  267.9 5.0 %copy-start.5 = (bf16[2,128,4,4,128]{4,1,3,2,0:T(8,128)(2,1)S(1)}, bf16[2,128,4,4,128]{4,1,3,2,0:T(8,128)(2,1)}, u32[]{:S(2)}) copy-start(bf16[2,128,4,4,128]{4,1,3,2,0:T(8,128)(2,1)} %get-tuple-element.458) | copy-start | bytes 3145732 | tf_op jit(solution)/shard_map/while
  272.9 2.2 copy-start.11
  272.9 3.5 copy-start.13
  277.0 3.2 copy-start.14
  295.0 4.4 copy-start.6
  297.6 5.2 %copy-start.2 = (f32[4,8,128,128,4]{3,2,4,1,0:T(8,128)}, f32[4,8,128,128,4]{3,2,4,1,0:T(8,128)S(1)}, u32[]{:S(2)}) copy-start(f32[4,8,128,128,4]{3,2,4,1,0:T(8,128)S(1)} %get-tuple-element.387) | copy-start | bytes 25165828 | tf_op jit(solution)/shard_map/while
  307.0 5.0 %copy-start.4 = (bf16[4,4,128,8,128]{2,4,1,3,0:T(8,128)(2,1)S(1)}, bf16[4,4,128,8,128]{2,4,1,3,0:T(8,128)(2,1)}, u32[]{:S(2)}) copy-start(bf16[4,4,128,8,128]{2,4,1,3,0:T(8,128)(2,1)} %copy-done.3) | copy-start | bytes 12582916 | tf_op jit(solution)/shard_map/while
  307.0 5.0 %copy-start.5 = (bf16[2,128,4,4,128]{4,1,3,2,0:T(8,128)(2,1)S(1)}, bf16[2,128,4,4,128]{4,1,3,2,0:T(8,128)(2,1)}, u32[]{:S(2)}) copy-start(bf16[2,128,4,4,128]{4,1,3,2,0:T(8,128)(2,1)} %get-tuple-element.458) | copy-start | bytes 3145732 | tf_op jit(solution)/shard_map/while
  312.0 2.2 copy-start.11
  312.0 3.4 copy-start.13
  316.0 3.2 copy-start.14
  319.2 7.8 %copy-start.17 = (s32[16]{0:T(128)S(1)}, s32[16]{0:T(128)}, u32[]{:S(2)}) copy-start(s32[16]{0:T(128)} %fusion.67) | copy-start | bytes 196
  340.2 152.9 %reduce-scatter.9.cloned.1.call-start = ((), (), s32[]{:S(2)}) async-start(), calls=%async_computation.8 | async-start | bytes 2359296 | tf_op jit(solution)/shard_map/reduce_scatter | solution.py:133
  348.0 13.2 %copy-start.15 = (bf16[2,128,4,4,128]{4,3,2,1,0:T(4,128)(2,1)S(1)}, bf16[2,128,4,4,128]{4,3,2,1,0:T(4,128)(2,1)}, u32[]{:S(2)}) copy-start(bf16[2,128,4,4,128]{4,3,2,1,0:T(4,128)(2,1)} %get-tuple-element.113) | copy-start | bytes 3145732
  357.3 5.6 %copy-start.10 = (bf16[256,2048]{1,0:T(8,128)(2,1)S(1)}, bf16[256,2048]{1,0:T(8,128)(2,1)}, u32[]{:S(2)}) copy-start(bf16[256,2048]{1,0:T(8,128)(2,1)} %copy-done.9) | copy-start | bytes 3145732
  361.3 131.8 %copy-start.1 = (bf16[1,256,2048]{2,1,0:T(8,128)(2,1)S(1)}, bf16[1,256,2048]{2,1,0:T(8,128)(2,1)}, u32[]{:S(2)}) copy-start(bf16[1,256,2048]{2,1,0:T(8,128)(2,1)} %param.18) | copy-start | bytes 3145732
  (5 other events, 7.8 us)
Sparse Core Ops, SparseCore 0:
  10.4 68.7 all-gather.2
  80.8 58.2 all-gather.4
  141.5 97.4 reduce-scatter.12
  242.4 69.3 reduce-scatter.10
  340.3 74.2 reduce-scatter.6
  419.2 73.8 reduce-scatter.8
